TPU v7x, 256 devices: a whole 4x4x8 slice. The times are simulated.
256 devices in a mesh: exp: 32 (over y, z_hi, core), hid: 8 (over z_lo, x).
Axes of the slice: x: 4, y: 4, z: 8 (z_hi: 4, z_lo: 2; z = z_hi * 2 + z_lo), core: 2. Of those that a mesh axis runs over, the one named last changes fastest.
Arguments:
- tokens: bfloat16 [1024, 2048], P(('exp', 'hid')), may hold values from -6 to 6
- grad_out: bfloat16 [1024, 2048], P(('exp', 'hid')), may hold values from -3 to 3
- router_logits: float32 [1024, 128], P(('exp', 'hid')), may hold values from -12 to 330
- selected: int32 [1024, 8], P(('exp', 'hid')), may hold values from 0 to 127, as said below
- router_w: bfloat16 [2048, 128], replicated, may hold values from -0.59765625 to 0.59765625
- w_gate: bfloat16 [256, 2048, 384], P(('exp', 'hid')), may hold values from -0.125 to 0.125
- w_up: bfloat16 [256, 2048, 384], P(('exp', 'hid')), may hold values from -0.125 to 0.125
- w_down: bfloat16 [256, 384, 2048], P(('exp', 'hid')), may hold values from -0.21875 to 0.21875
Outputs:
- x_grad: bfloat16 [1024, 2048], P(('exp', 'hid'))
- router_grad: float32 [2048, 128], P(('exp', 'hid'))
Inputs may be any that keep to these rules, and one draw needn't show every extreme that they name: `selected`: each row names 8 different experts; within each aligned block of 32 rows (the tokens of one index of exp) no expert is named by more than 4 rows, and in every block some expert is named by exactly 4 rows.
All inputs are finite; a program needn't handle non-finite values.
Results may differ from a plain program's by a relative error of at most 0.0075.
Values may be sent and summed in bfloat16 or wider, within the bound.
A program may use at most 64 MiB of HBM per device.

v0:
```python
import jax
import jax.numpy as jnp
from jax import lax
from jax.sharding import PartitionSpec as P


def softmax_rows(values):
    top_val = jnp.max(values, axis=-1, keepdims=True)
    raised = jnp.exp(values - top_val)
    return raised / jnp.sum(raised, axis=-1, keepdims=True)


def combine_table(logits, chosen, expert_count):
    picked = jnp.take_along_axis(logits, chosen, axis=1)
    weights = softmax_rows(picked)
    expert_ids = jnp.arange(expert_count, dtype=jnp.int32)
    matched = (chosen[:, :, None] == expert_ids[None, None, :]).astype(jnp.float32)
    return jnp.sum(weights[:, :, None] * matched, axis=1).astype(jnp.bfloat16)


CAP = 4


def slot_rows(column, group_rows):
    shaped = column.reshape(column.shape[:-1] + (-1, group_rows))
    place = jnp.arange(group_rows, dtype=jnp.int32)
    key = jnp.where(shaped != 0, 2 * group_rows - place, -place)
    return lax.top_k(key, CAP)[1]


def dense_terms(x_rows, g_rows, w_gate, w_up, w_down):
    gate_pre = jnp.einsum("td,udf->utf", x_rows, w_gate, preferred_element_type=jnp.float32)
    up_pre = jnp.einsum("td,udf->utf", x_rows, w_up, preferred_element_type=jnp.float32)
    back_grad = jnp.einsum("td,ufd->utf", g_rows, w_down, preferred_element_type=jnp.float32)
    sig_gate = jax.nn.sigmoid(gate_pre)
    act_gate = gate_pre * sig_gate
    score_part = jnp.sum(act_gate * up_pre * back_grad, axis=2).T
    return (score_part, gate_pre, up_pre, back_grad)


def sparse_terms(gate_pre, up_pre, back_grad, column, w_gate, w_up, group_rows):
    picked = slot_rows(column, group_rows)
    groups = picked.shape[1]
    starts = (jnp.arange(groups, dtype=jnp.int32) * group_rows)[None, :, None]
    rows = (picked + starts).reshape(picked.shape[0], -1)
    take = lambda a: jnp.take_along_axis(a, rows[:, :, None], axis=1)
    gate_s, up_s, back_s = (take(gate_pre), take(up_pre), take(back_grad))
    col_s = jnp.take_along_axis(column, rows, axis=1)
    sig_gate = jax.nn.sigmoid(gate_s)
    act_gate = gate_s * sig_gate
    weighted = col_s[:, :, None] * back_s
    grad_gate = (weighted * up_s * sig_gate * (1.0 + gate_s * (1.0 - sig_gate))).astype(
        jnp.bfloat16
    )
    grad_up = (weighted * act_gate).astype(jnp.bfloat16)
    part = jnp.einsum("usf,udf->usd", grad_gate, w_gate, preferred_element_type=jnp.float32)
    part = part + jnp.einsum("usf,udf->usd", grad_up, w_up, preferred_element_type=jnp.float32)
    return part.reshape(part.shape[0], groups, CAP, part.shape[-1])


def on_device(tokens, grad_out, router_logits, selected, router_w, w_gate, w_up, w_down):
    tok_local, model_width = tokens.shape
    unit_count = w_gate.shape[0]
    expert_count = router_logits.shape[1]
    spread_exp = lax.axis_size("exp")
    spread_hid = lax.axis_size("hid")
    group_rows = spread_hid * tok_local
    own_exp = lax.axis_index("exp")
    own_hid = lax.axis_index("hid")
    own_block = lax.axis_index(("exp", "hid"))
    unit_expert = (own_block * unit_count + jnp.arange(unit_count, dtype=jnp.int32)) // 2
    expert_ids = jnp.arange(expert_count, dtype=jnp.int32)
    unit_pick = (expert_ids[:, None] == unit_expert[None, :]).astype(jnp.bfloat16)
    combine = combine_table(router_logits, selected, expert_count)
    packed = jnp.concatenate([tokens, grad_out, combine], axis=1)
    gathered = lax.all_gather(
        lax.all_gather(packed, "hid", axis=0, tiled=True), "exp", axis=0, tiled=True
    )
    combine_all = gathered[:, 2 * model_width :]
    score_part, gate_pre, up_pre, back_grad = dense_terms(
        gathered[:, :model_width], gathered[:, model_width : 2 * model_width], w_gate, w_up, w_down
    )
    column = jnp.dot(combine_all, unit_pick, preferred_element_type=jnp.float32).T
    part = sparse_terms(gate_pre, up_pre, back_grad, column, w_gate, w_up, group_rows)
    lane = 128
    score_grp = jnp.swapaxes(
        score_part.T.reshape(unit_count, spread_exp, CAP, group_rows // CAP), 0, 1
    )
    score_grp = jnp.pad(score_grp, ((0, 0), (0, 0), (0, 0), (0, lane - group_rows // CAP)))
    sent = jnp.concatenate([jnp.swapaxes(part, 0, 1), score_grp], axis=3)
    arrived_part = lax.all_to_all(sent, "exp", split_axis=0, concat_axis=0, tiled=True)
    sender_block = (jnp.arange(spread_exp, dtype=jnp.int32) * spread_hid + own_hid)[:, None]
    sender_expert = (
        sender_block * unit_count + jnp.arange(unit_count, dtype=jnp.int32)[None, :]
    ) // 2
    own_combine = lax.dynamic_slice_in_dim(combine_all, own_exp * group_rows, group_rows, 0)
    sender_pick = (expert_ids[:, None] == sender_expert.reshape(1, -1)).astype(jnp.bfloat16)
    sender_column = jnp.dot(own_combine, sender_pick, preferred_element_type=jnp.float32).T
    sender_rows = slot_rows(sender_column, group_rows).reshape(-1)
    place = (sender_rows[:, None] == jnp.arange(group_rows, dtype=jnp.int32)[None, :]).astype(
        jnp.float32
    )
    group_sum = jnp.einsum(
        "sj,sd->jd",
        place,
        arrived_part[..., :model_width].reshape(-1, model_width),
        precision=lax.Precision.HIGHEST,
        preferred_element_type=jnp.float32,
    )
    got_scores = arrived_part[..., model_width : model_width + group_rows // CAP]
    got_scores = got_scores.reshape(spread_exp, unit_count, spread_hid, tok_local)
    score_cols = spread_exp * unit_count
    score_width = -(-score_cols // lane) * lane
    hid_scores = jnp.transpose(got_scores, (2, 3, 0, 1)).reshape(spread_hid, tok_local, score_cols)
    hid_scores = jnp.pad(hid_scores, ((0, 0), (0, 0), (0, score_width - score_cols)))
    hid_sent = jnp.concatenate(
        [group_sum.reshape(spread_hid, tok_local, model_width), hid_scores], axis=2
    )
    spread_rows = lax.all_to_all(hid_sent, "hid", split_axis=0, concat_axis=0, tiled=True)
    input_sum = jnp.sum(spread_rows[..., :model_width], axis=0)
    own_scores = spread_rows[..., model_width : model_width + score_cols]
    own_scores = own_scores.reshape(spread_hid, tok_local, spread_exp, unit_count)
    unit_scores = jnp.transpose(own_scores, (1, 2, 0, 3)).reshape(tok_local, -1)
    expert_scores = jnp.sum(unit_scores.reshape(tok_local, expert_count, 2), axis=2)
    probs_all = softmax_rows(router_logits)
    mean_score = jnp.sum(probs_all * expert_scores, axis=1, keepdims=True)
    logit_grad = (probs_all * (expert_scores - mean_score)).astype(jnp.bfloat16)
    devices = spread_exp * spread_hid
    logit_all = lax.all_to_all(
        jnp.broadcast_to(logit_grad[None], (devices,) + logit_grad.shape),
        ("exp", "hid"),
        0,
        0,
        tiled=True,
    ).reshape(-1, expert_count)
    grad_rows = model_width // devices
    token_cols = lax.dynamic_slice_in_dim(gathered, own_block * grad_rows, grad_rows, 1)
    router_grad = jnp.einsum("tc,te->ce", token_cols, logit_all, preferred_element_type=jnp.float32)
    router_part = jnp.einsum("te,de->td", logit_grad, router_w, preferred_element_type=jnp.float32)
    x_grad = (input_sum + router_part).astype(jnp.bfloat16)
    return (x_grad, router_grad)


def solution(mesh):
    placed = (
        P(("exp", "hid"), None),
        P(("exp", "hid"), None),
        P(("exp", "hid"), None),
        P(("exp", "hid"), None),
        P(),
        P(("exp", "hid"), None, None),
        P(("exp", "hid"), None, None),
        P(("exp", "hid"), None, None),
    )
    return jax.shard_map(
        on_device,
        mesh=mesh,
        in_specs=placed,
        out_specs=(P(("exp", "hid"), None), P(("exp", "hid"), None)),
        check_vma=False,
    )
```

profile of v0, /device:TPU:1, one launch (start us, length us, event | category | flops | bytes accessed | tf_op | source)
XLA Modules:
  0.0 250.1 jit_solution(14854167661253626803)
XLA Ops:
  7.3 0.8 bitcast_or_fusion
  8.1 1.4 gather_fusion.1
  9.7 0.1 fusion.62
  9.8 0.2 fusion.47
  10.2 24.1 %all-gather = bf16[8,4,4224]{2,1,0:T(4,128)(2,1)S(1)} all-gather(bf16[1,4,4224]{2,1,0:T(4,128)(2,1)S(1)} %maximum_bitcast_fusion), channel_id=1, replica_groups=mesh['exp'=32,'hid'=8] {'hid'}, dimensions={0}, use_global_device_ids=true | all-gather | bytes 304128 | tf_op jit(solution)/shard_map/all_gather | solution.py:77
  34.3 0.8 reshape.445
  35.1 85.0 %all-gather.3.cloned.1.call-done = bf16[1024,4224]{1,0:T(8,128)(2,1)} async-done(((bf16[32,4224]{1,0:T(8,128)(2,1)}), bf16[1024,4224]{1,0:T(8,128)(2,1)}) %all-gather.3.cloned.1.call-update) | async-done | bytes 8650768 | tf_op jit(solution)/shard_map/all_gather | solution.py:76
  120.1 1.1 fusion.43
  121.5 0.8 top_k.24
  122.4 0.1 reshape.376
  122.7 0.6 reshape.373
  123.3 1.5 gather_fusion
  124.8 5.3 %fusion.4 = f32[1024,384]{0,1:T(8,128)} fusion(bf16[1024,4224]{1,0:T(8,128)(2,1)} %all-gather.3.cloned.1.call-done, bf16[1,2048,384]{2,1,0:T(8,128)(2,1)S(1)} %copy-done.2), kind=kOutput, calls=%fused_computation.9 | convolution fusion | flops 1610612736 | bytes 7340032 | tf_op jit(solution)/shard_map/td,udf->utf/dot_general | solution.py:33
  130.0 1.9 copy.90
  131.9 5.2 %fusion.2 = f32[1024,384]{0,1:T(8,128)} fusion(bf16[1024,4224]{1,0:T(8,128)(2,1)} %all-gather.3.cloned.1.call-done, bf16[1,2048,384]{2,1,0:T(8,128)(2,1)S(1)} %copy-done), kind=kOutput, calls=%fused_computation.7 | convolution fusion | flops 1610612736 | bytes 7340032 | tf_op jit(solution)/shard_map/td,udf->utf/dot_general | solution.py:32
  137.1 3.1 %copy.91 = f32[1024,384]{1,0:T(8,128)} copy(f32[1024,384]{0,1:T(8,128)} %fusion.2) | data formatting | bytes 3145728 | tf_op jit(solution)/shard_map/jit(take_along_axis)/Arg_0.9 | solution.py:46
  140.2 1.4 gather_fusion.3
  141.6 2.4 gather_fusion.4
  144.0 6.2 %fusion.7 = (f32[1024]{0:T(1024)S(1)}, f32[1024,384]{0,1:T(8,128)}) fusion(f32[1024,384]{0,1:T(8,128)S(1)} %copy-done.4, f32[1024,384]{0,1:T(8,128)} %fusion.2, bf16[1,384,2048]{2,1,0:T(8,128)(2,1)} %param.17, bf16[1024,4224]{1,0:T(8,128)(2,1)} %all-gather.3.cloned.1.call-done), kind=kOutput, calls=%fused_computation.15 | convolution fusion | flops 1613364224 | bytes 10489856 | tf_op jit(solution)/shard_map/td,ufd->utf/dot_general | solution.py:34
  150.2 0.1 transpose_reshape.7
  150.3 0.6 pad_bitcast_fusion
  150.9 1.9 copy.89
  152.8 0.8 gather_fusion.2
  153.6 0.7 and_select_fusion
  154.3 1.7 fusion.11
  156.0 0.7 convolution_add_fusion
  156.7 1.3 transpose_reshape.6
  158.0 2.6 %pad_maximum_fusion = f32[32,1,4,2176]{3,2,1,0:T(4,128)} fusion(f32[32,1,4,128]{3,2,1,0:T(4,128)S(1)} %copy-done.6, f32[32,1,4,2048]{3,2,1,0:T(4,128)} %bitcast.146), kind=kLoop, calls=%fused_computation.28 | loop fusion | flops 278528 | bytes 2228224 | tf_op jit(solution)/shard_map/concatenate | solution.py:90
  160.5 10.4 %all-to-all-start = ((f32[32,1,4,2176]{3,2,1,0:T(4,128)}), f32[32,1,4,2176]{3,2,1,0:T(4,128)S(1)}, u32[]{:S(2)}, u32[]{:S(2)}) async-start(f32[32,1,4,2176]{3,2,1,0:T(4,128)} %pad_maximum_fusion), calls=%async_computation | async-start | bytes 2228224 | tf_op jit(solution)/shard_map/all_to_all | solution.py:91
  171.0 0.2 fusion.18
  171.2 0.8 top_k.17
  172.2 28.5 %all-to-all-done = f32[32,1,4,2176]{3,2,1,0:T(4,128)S(1)} async-done(((f32[32,1,4,2176]{3,2,1,0:T(4,128)}), f32[32,1,4,2176]{3,2,1,0:T(4,128)S(1)}, u32[]{:S(2)}, u32[]{:S(2)}) %all-to-all-start) | async-done | bytes 1114144 | tf_op jit(solution)/shard_map/all_to_all | solution.py:91
  200.8 1.2 slice.45
  202.0 1.6 reshape.463
  203.6 0.5 fusion.38
  204.2 0.8 copy.96
  205.0 4.0 %all-to-all-start.1 = ((f32[8,4,2176]{2,1,0:T(4,128)}), f32[8,4,2176]{2,1,0:T(4,128)S(1)}, u32[]{:S(2)}, u32[]{:S(2)}) async-start(f32[8,4,2176]{2,1,0:T(4,128)} %copy.96), calls=%async_computation.1 | async-start | bytes 557056 | tf_op jit(solution)/shard_map/all_to_all | solution.py:119
  209.0 0.1 reduce_max.19
  209.1 0.2 fusion.49
  209.3 5.8 %all-to-all-done.1 = f32[8,4,2176]{2,1,0:T(4,128)S(1)} async-done(((f32[8,4,2176]{2,1,0:T(4,128)}), f32[8,4,2176]{2,1,0:T(4,128)S(1)}, u32[]{:S(2)}, u32[]{:S(2)}) %all-to-all-start.1) | async-done | bytes 278560 | tf_op jit(solution)/shard_map/all_to_all | solution.py:119
  215.2 0.1 copy.97
  215.3 0.2 reduce_sum.68
  215.5 0.2 multiply_reduce_fusion
  215.8 0.8 broadcast_in_dim.59
  216.6 9.1 %all-to-all-start.2 = ((bf16[256,4,128]{2,1,0:T(4,128)(2,1)}), bf16[256,4,128]{2,1,0:T(4,128)(2,1)S(1)}, u32[]{:S(2)}, u32[]{:S(2)}) async-start(bf16[256,4,128]{2,1,0:T(4,128)(2,1)} %broadcast_in_dim.59), calls=%async_computation.2 | async-start | bytes 524288 | tf_op jit(solution)/shard_map/all_to_all | solution.py:129
  225.8 0.9 fusion.6
  226.6 14.8 %all-to-all-done.2 = bf16[256,4,128]{2,1,0:T(4,128)(2,1)S(1)} async-done(((bf16[256,4,128]{2,1,0:T(4,128)(2,1)}), bf16[256,4,128]{2,1,0:T(4,128)(2,1)S(1)}, u32[]{:S(2)}, u32[]{:S(2)}) %all-to-all-start.2) | async-done | bytes 262176 | tf_op jit(solution)/shard_map/all_to_all | solution.py:129
  241.4 1.9 fusion.19
  (59 shorter events, 1.5 us)
Async XLA Ops:
  7.2 124.7 %copy-start = (bf16[1,2048,384]{2,1,0:T(8,128)(2,1)S(1)}, bf16[1,2048,384]{2,1,0:T(8,128)(2,1)}, u32[]{:S(2)}) copy-start(bf16[1,2048,384]{2,1,0:T(8,128)(2,1)} %param.15) | copy-start | bytes 4718596
  7.2 2.5 copy-start.7
  7.2 3.0 %copy-start.8 = (bf16[4,2048]{1,0:T(4,128)(2,1)S(1)}, bf16[4,2048]{1,0:T(4,128)(2,1)}, u32[]{:S(2)}) copy-start(bf16[4,2048]{1,0:T(4,128)(2,1)} %param.11) | copy-start | bytes 49156
  7.2 3.0 %copy-start.9 = (bf16[4,2048]{1,0:T(4,128)(2,1)S(1)}, bf16[4,2048]{1,0:T(4,128)(2,1)}, u32[]{:S(2)}) copy-start(bf16[4,2048]{1,0:T(4,128)(2,1)} %param.10) | copy-start | bytes 49156
  7.2 112.9 %all-gather.3.cloned.1.call-start = ((), (), s32[]{:S(2)}) async-start(), calls=%async_computation.3 | async-start | bytes 8921088 | tf_op jit(solution)/shard_map/all_gather | solution.py:76
  9.6 115.2 %copy-start.2 = (bf16[1,2048,384]{2,1,0:T(8,128)(2,1)S(1)}, bf16[1,2048,384]{2,1,0:T(8,128)(2,1)}, u32[]{:S(2)}) copy-start(bf16[1,2048,384]{2,1,0:T(8,128)(2,1)} %param.16) | copy-start | bytes 4718596
  141.6 2.4 copy-start.4
  154.3 1.7 copy-start.3
  156.7 1.3 copy-start.6
  160.5 10.4 %slice-start = ((bf16[1024,4224]{1,0:T(8,128)(2,1)}), bf16[1024,128]{1,0:T(8,128)(2,1)S(1)}, s32[]{:S(2)}) async-start(bf16[1024,4224]{1,0:T(8,128)(2,1)} %all-gather.3.cloned.1.call-done), calls=%async_computation.4 | async-start | bytes 524288 | tf_op jit(solution)/shard_map/slice | solution.py:79
  160.5 40.2 %all-to-all-start = ((f32[32,1,4,2176]{3,2,1,0:T(4,128)}), f32[32,1,4,2176]{3,2,1,0:T(4,128)S(1)}, u32[]{:S(2)}, u32[]{:S(2)}) async-start(f32[32,1,4,2176]{3,2,1,0:T(4,128)} %pad_maximum_fusion), calls=%async_computation | async-start | bytes 2228224 | tf_op jit(solution)/shard_map/all_to_all | solution.py:91
  203.6 5.4 %copy-start.1 = (f32[4,128]{1,0:T(4,128)S(1)}, f32[4,128]{1,0:T(4,128)}, u32[]{:S(2)}) copy-start(f32[4,128]{1,0:T(4,128)} %param.12) | copy-start | bytes 6148
  204.1 21.6 %copy-start.5 = (bf16[2048,128]{1,0:T(8,128)(2,1)S(1)}, bf16[2048,128]{1,0:T(8,128)(2,1)}, u32[]{:S(2)}) copy-start(bf16[2048,128]{1,0:T(8,128)(2,1)} %param.14) | copy-start | bytes 1572868
  205.0 10.2 %all-to-all-start.1 = ((f32[8,4,2176]{2,1,0:T(4,128)}), f32[8,4,2176]{2,1,0:T(4,128)S(1)}, u32[]{:S(2)}, u32[]{:S(2)}) async-start(f32[8,4,2176]{2,1,0:T(4,128)} %copy.96), calls=%async_computation.1 | async-start | bytes 557056 | tf_op jit(solution)/shard_map/all_to_all | solution.py:119
  216.6 24.8 %all-to-all-start.2 = ((bf16[256,4,128]{2,1,0:T(4,128)(2,1)}), bf16[256,4,128]{2,1,0:T(4,128)(2,1)S(1)}, u32[]{:S(2)}, u32[]{:S(2)}) async-start(bf16[256,4,128]{2,1,0:T(4,128)(2,1)} %broadcast_in_dim.59), calls=%async_computation.2 | async-start | bytes 524288 | tf_op jit(solution)/shard_map/all_to_all | solution.py:129
Sparse Core Ops, SparseCore 0:
  35.2 84.8 all-gather.2
where the time goes:
time: 251 us; the launch traced here: 250 us
  waiting for transfers between devices  134 us (53%)
  blocking collectives  24.1 us (10%)
  starting transfers between devices  23.6 us (9%)
  matrix products  23.5 us (9%)
  local copies, waits for them, and re-layouts  23.4 us (9%)
  between operations  14.4 us (6%)
  other arithmetic  7.08 us (3%)
    all_gather x1, waiting for transfers between devices, on_device(): lax.all_gather(lax.all_gather(packed, 'hid', axis=0, tiled=True), 'exp',...  85 us
    all_to_all x1, waiting for transfers between devices, on_device(): lax.all_to_all(sent, 'exp', split_axis=0, concat_axis=0, tiled=True)  28.5 us
    all_gather x1, blocking collectives, on_device(): lax.all_gather(packed, 'hid', axis=0, tiled=True)  24.1 us
    all_to_all x1, waiting for transfers between devices, on_device(): lax.all_to_all(jnp.broadcast_to(logit_grad[None], (devices,) + logit_grad...  14.8 us
    all_to_all x1, starting transfers between devices, on_device(): lax.all_to_all(sent, 'exp', split_axis=0, concat_axis=0, tiled=True)  10.4 us
    all_to_all x1, starting transfers between devices, on_device(): lax.all_to_all(jnp.broadcast_to(logit_grad[None], (devices,) + logit_grad...  9.1 us
    another operation x3, local copies, waits for them, and re-layouts, sparse_terms(): take = lambda a: jnp.take_along_axis(a, rows[:, :, None], axis=1)  6.86 us
    dot_general x1, matrix products, dense_terms(): jnp.einsum('td,ufd->utf', g_rows, w_down, preferred_element_type=jnp.floa...  6.17 us
  transfers between devices with their start and end apart: 4, of which 4 were waited for; matrix products, arithmetic and copies ran while one was open for 1% of the time, Pallas kernels for 0%

commit v1 on v0

--- a/solution.py
+++ b/solution.py
@@ -73,8 +73,14 @@
     unit_pick = (expert_ids[:, None] == unit_expert[None, :]).astype(jnp.bfloat16)
     combine = combine_table(router_logits, selected, expert_count)
     packed = jnp.concatenate([tokens, grad_out, combine], axis=1)
-    gathered = lax.all_gather(
-        lax.all_gather(packed, "hid", axis=0, tiled=True), "exp", axis=0, tiled=True
+    gathered = jnp.concatenate(
+        lax.all_to_all(
+            jnp.stack([lax.all_gather(packed, "hid", axis=0, tiled=True)] * lax.axis_size("exp")),
+            "exp",
+            0,
+            0,
+        ),
+        axis=0,
     )
     combine_all = gathered[:, 2 * model_width :]
     score_part, gate_pre, up_pre, back_grad = dense_terms(

time: 251 us -> 360 us (1.43)
  waiting for transfers between devices: 134 us -> 236 us
  starting transfers between devices: 23.6 us -> 39.8 us
  between operations: 14.4 us -> 0.98 us
    all_to_all x0 -> x1, waiting for transfers between devices: none -> 191 us  [on_device(): lax.all_to_all(jnp.stack([lax.all_gather(packed, 'hid', axis=0, tiled=Tru...]
    all_gather x1 -> x0, waiting for transfers between devices: 85 us -> none  [on_device(): lax.all_gather(lax.all_gather(packed, 'hid', axis=0, tiled=True), 'exp',...]
    all_to_all x0 -> x1, starting transfers between devices: none -> 17.2 us  [on_device(): lax.all_to_all(jnp.stack([lax.all_gather(packed, 'hid', axis=0, tiled=Tru...]
    all_to_all x1, starting transfers between devices: 10.4 us -> 5.66 us  [on_device(): lax.all_to_all(sent, 'exp', split_axis=0, concat_axis=0, tiled=True)]
    all_to_all x1, waiting for transfers between devices: 28.5 us -> 24.4 us  [on_device(): lax.all_to_all(sent, 'exp', split_axis=0, concat_axis=0, tiled=True)]
    all_to_all x1, starting transfers between devices: 4.05 us -> 7.96 us  [on_device(): lax.all_to_all(hid_sent, 'hid', split_axis=0, concat_axis=0, tiled=True)]
    another operation x0 -> x1, local copies, waits for them, and re-layouts: none -> 3.88 us  [on_device(): jnp.stack([lax.all_gather(packed, 'hid', axis=0, tiled=True)] * lax.axis_...]
where the time goes in v1:
time: 360 us; the launch traced here: 359 us
  waiting for transfers between devices  236 us (66%)
  starting transfers between devices  39.8 us (11%)
  local copies, waits for them, and re-layouts  26.1 us (7%)
  matrix products  24.2 us (7%)
  blocking collectives  24.1 us (7%)
  other arithmetic  7.74 us (2%)
    all_to_all x1, waiting for transfers between devices, on_device(): lax.all_to_all(jnp.stack([lax.all_gather(packed, 'hid', axis=0, tiled=Tru...  191 us
    all_to_all x1, waiting for transfers between devices, on_device(): lax.all_to_all(sent, 'exp', split_axis=0, concat_axis=0, tiled=True)  24.4 us
    all_gather x1, blocking collectives, on_device(): lax.all_gather(packed, 'hid', axis=0, tiled=True)  24.1 us
    all_to_all x1, starting transfers between devices, on_device(): lax.all_to_all(jnp.stack([lax.all_gather(packed, 'hid', axis=0, tiled=Tru...  17.2 us
    all_to_all x1, waiting for transfers between devices, on_device(): lax.all_to_all(jnp.broadcast_to(logit_grad[None], (devices,) + logit_grad...  14.8 us
    all_to_all x1, starting transfers between devices, on_device(): lax.all_to_all(jnp.broadcast_to(logit_grad[None], (devices,) + logit_grad...  8.95 us
    all_to_all x1, starting transfers between devices, on_device(): lax.all_to_all(hid_sent, 'hid', split_axis=0, concat_axis=0, tiled=True)  7.96 us
  transfers between devices with their start and end apart: 4, of which 4 were waited for; matrix products, arithmetic and copies ran while one was open for 1% of the time, Pallas kernels for 0%

profile of v1, /device:TPU:1, one launch (start us, length us, event | category | flops | bytes accessed | tf_op | source)
XLA Modules:
  0.0 359.1 jit_solution(4121491500593864533)
XLA Ops:
  0.7 0.8 bitcast_or_fusion
  1.6 1.4 gather_fusion.1
  3.2 0.2 fusion.47
  3.6 24.1 %all-gather = bf16[8,4,4224]{2,1,0:T(4,128)(2,1)S(1)} all-gather(bf16[1,4,4224]{2,1,0:T(4,128)(2,1)S(1)} %maximum_bitcast_fusion), channel_id=1, replica_groups=mesh['exp'=32,'hid'=8] {'hid'}, dimensions={0}, use_global_device_ids=true | all-gather | bytes 304128 | tf_op jit(solution)/shard_map/all_gather | solution.py:78
  27.8 3.9 %stack.2 = bf16[32,32,4224]{2,1,0:T(8,128)(2,1)} broadcast(bf16[32,4224]{1,0:T(8,128)(2,1)S(1)} %reshape.451), dimensions={1,2} | broadcast | bytes 8921088 | tf_op jit(solution)/shard_map/stack | solution.py:78
  31.7 17.2 %all-to-all-start = ((bf16[32,32,4224]{2,1,0:T(8,128)(2,1)}), bf16[32,32,4224]{2,1,0:T(8,128)(2,1)}, u32[]{:S(2)}, u32[]{:S(2)}) async-start(bf16[32,32,4224]{2,1,0:T(8,128)(2,1)} %stack.2), calls=%async_computation | async-start | bytes 17301504 | tf_op jit(solution)/shard_map/all_to_all | solution.py:77
  49.0 191.1 %all-to-all-done = bf16[32,32,4224]{2,1,0:T(8,128)(2,1)} async-done(((bf16[32,32,4224]{2,1,0:T(8,128)(2,1)}), bf16[32,32,4224]{2,1,0:T(8,128)(2,1)}, u32[]{:S(2)}, u32[]{:S(2)}) %all-to-all-start) | async-done | bytes 8650784 | tf_op jit(solution)/shard_map/all_to_all | solution.py:77
  240.1 1.1 fusion.43
  241.5 0.8 top_k.24
  242.5 0.6 reshape.380
  243.2 0.7 reshape.379
  243.9 5.3 %fusion.4 = f32[1024,384]{0,1:T(8,128)} fusion(bf16[1024,4224]{1,0:T(8,128)(2,1)} %bitcast.2, bf16[1,2048,384]{2,1,0:T(8,128)(2,1)S(1)} %copy-done.2), kind=kOutput, calls=%fused_computation.9 | convolution fusion | flops 1610612736 | bytes 7340032 | tf_op jit(solution)/shard_map/td,udf->utf/dot_general | solution.py:33
  249.1 5.3 %fusion.2 = f32[1024,384]{0,1:T(8,128)} fusion(bf16[1024,4224]{1,0:T(8,128)(2,1)} %bitcast.2, bf16[1,2048,384]{2,1,0:T(8,128)(2,1)S(1)} %copy-done), kind=kOutput, calls=%fused_computation.7 | convolution fusion | flops 1610612736 | bytes 7340032 | tf_op jit(solution)/shard_map/td,udf->utf/dot_general | solution.py:32
  254.4 1.7 copy.90
  256.1 1.9 copy.91
  258.0 6.7 %fusion.7 = (f32[1024]{0:T(1024)S(1)}, f32[1024,384]{0,1:T(8,128)}) fusion(f32[1024,384]{0,1:T(8,128)} %fusion.4, f32[1024,384]{0,1:T(8,128)} %fusion.2, bf16[1,384,2048]{2,1,0:T(8,128)(2,1)} %param.17, bf16[1024,4224]{1,0:T(8,128)(2,1)} %bitcast.2), kind=kOutput, calls=%fused_computation.15 | convolution fusion | flops 1613364224 | bytes 10489856 | tf_op jit(solution)/shard_map/td,ufd->utf/dot_general | solution.py:34
  264.8 0.6 pad_bitcast_fusion
  265.5 2.9 gather_fusion.3
  268.4 0.8 gather_fusion.4
  269.1 1.9 copy.89
  271.0 0.8 gather_fusion.2
  271.8 0.7 fusion.50
  272.5 1.0 gather_fusion
  273.4 0.7 and_select_fusion
  274.1 1.8 fusion.11
  275.9 0.7 convolution_add_fusion
  276.6 1.3 transpose_reshape.6
  277.9 2.6 pad_maximum_fusion
  280.4 5.7 %all-to-all-start.1 = ((f32[32,1,4,2176]{3,2,1,0:T(4,128)}), f32[32,1,4,2176]{3,2,1,0:T(4,128)S(1)}, u32[]{:S(2)}, u32[]{:S(2)}) async-start(f32[32,1,4,2176]{3,2,1,0:T(4,128)} %pad_maximum_fusion), calls=%async_computation.1 | async-start | bytes 2228224 | tf_op jit(solution)/shard_map/all_to_all | solution.py:97
  286.1 1.0 slice.42
  287.1 0.2 fusion.18
  287.4 0.8 top_k.17
  288.4 24.4 %all-to-all-done.1 = f32[32,1,4,2176]{3,2,1,0:T(4,128)S(1)} async-done(((f32[32,1,4,2176]{3,2,1,0:T(4,128)}), f32[32,1,4,2176]{3,2,1,0:T(4,128)S(1)}, u32[]{:S(2)}, u32[]{:S(2)}) %all-to-all-start.1) | async-done | bytes 1114144 | tf_op jit(solution)/shard_map/all_to_all | solution.py:97
  312.9 1.2 slice.45
  314.1 1.6 reshape.469
  315.7 0.5 fusion.38
  316.2 0.8 copy.96
  317.0 8.0 %all-to-all-start.2 = ((f32[8,4,2176]{2,1,0:T(4,128)}), f32[8,4,2176]{2,1,0:T(4,128)S(1)}, u32[]{:S(2)}, u32[]{:S(2)}) async-start(f32[8,4,2176]{2,1,0:T(4,128)} %copy.96), calls=%async_computation.2 | async-start | bytes 557056 | tf_op jit(solution)/shard_map/all_to_all | solution.py:125
  325.1 0.2 fusion.49
  325.3 5.8 %all-to-all-done.2 = f32[8,4,2176]{2,1,0:T(4,128)S(1)} async-done(((f32[8,4,2176]{2,1,0:T(4,128)}), f32[8,4,2176]{2,1,0:T(4,128)S(1)}, u32[]{:S(2)}, u32[]{:S(2)}) %all-to-all-start.2) | async-done | bytes 278560 | tf_op jit(solution)/shard_map/all_to_all | solution.py:125
  331.1 0.1 copy.97
  331.3 0.2 reduce_sum.68
  331.5 0.2 multiply_reduce_fusion
  331.8 0.8 broadcast_in_dim.59
  332.6 8.9 %all-to-all-start.3 = ((bf16[256,4,128]{2,1,0:T(4,128)(2,1)}), bf16[256,4,128]{2,1,0:T(4,128)(2,1)S(1)}, u32[]{:S(2)}, u32[]{:S(2)}) async-start(bf16[256,4,128]{2,1,0:T(4,128)(2,1)} %broadcast_in_dim.59), calls=%async_computation.3 | async-start | bytes 524288 | tf_op jit(solution)/shard_map/all_to_all | solution.py:135
  341.6 0.9 fusion.6
  342.5 14.8 %all-to-all-done.3 = bf16[256,4,128]{2,1,0:T(4,128)(2,1)S(1)} async-done(((bf16[256,4,128]{2,1,0:T(4,128)(2,1)}), bf16[256,4,128]{2,1,0:T(4,128)(2,1)S(1)}, u32[]{:S(2)}, u32[]{:S(2)}) %all-to-all-start.3) | async-done | bytes 262176 | tf_op jit(solution)/shard_map/all_to_all | solution.py:135
  357.2 1.9 fusion.19
  (62 shorter events, 1.9 us)
Async XLA Ops:
  0.6 248.5 %copy-start = (bf16[1,2048,384]{2,1,0:T(8,128)(2,1)S(1)}, bf16[1,2048,384]{2,1,0:T(8,128)(2,1)}, u32[]{:S(2)}) copy-start(bf16[1,2048,384]{2,1,0:T(8,128)(2,1)} %param.15) | copy-start | bytes 4718596
  0.6 2.4 copy-start.7
  0.7 2.9 copy-start.8
  0.7 2.9 copy-start.9
  31.7 212.2 %copy-start.2 = (bf16[1,2048,384]{2,1,0:T(8,128)(2,1)S(1)}, bf16[1,2048,384]{2,1,0:T(8,128)(2,1)}, u32[]{:S(2)}) copy-start(bf16[1,2048,384]{2,1,0:T(8,128)(2,1)} %param.16) | copy-start | bytes 4718596
  31.7 208.4 %all-to-all-start = ((bf16[32,32,4224]{2,1,0:T(8,128)(2,1)}), bf16[32,32,4224]{2,1,0:T(8,128)(2,1)}, u32[]{:S(2)}, u32[]{:S(2)}) async-start(bf16[32,32,4224]{2,1,0:T(8,128)(2,1)} %stack.2), calls=%async_computation | async-start | bytes 17301504 | tf_op jit(solution)/shard_map/all_to_all | solution.py:77
  49.0 192.5 %copy-start.10 = (s32[32]{0:T(128)}, s32[32]{0:T(128)S(1)}, u32[]{:S(2)}) copy-start(s32[32]{0:T(128)S(1)} %get-tuple-element.18) | copy-start | bytes 388
  249.1 5.3 %copy-start.4 = (f32[1024,384]{0,1:T(8,128)S(1)}, f32[1024,384]{0,1:T(8,128)}, u32[]{:S(2)}) copy-start(f32[1024,384]{0,1:T(8,128)} %fusion.4) | copy-start | bytes 4718596
  274.1 1.8 copy-start.3
  276.6 1.3 copy-start.6
  280.4 6.7 %copy-start.11 = (s32[32]{0:T(128)S(1)}, s32[32]{0:T(128)}, u32[]{:S(2)}) copy-start(s32[32]{0:T(128)} %copy-done.10) | copy-start | bytes 388
  280.4 32.4 %all-to-all-start.1 = ((f32[32,1,4,2176]{3,2,1,0:T(4,128)}), f32[32,1,4,2176]{3,2,1,0:T(4,128)S(1)}, u32[]{:S(2)}, u32[]{:S(2)}) async-start(f32[32,1,4,2176]{3,2,1,0:T(4,128)} %pad_maximum_fusion), calls=%async_computation.1 | async-start | bytes 2228224 | tf_op jit(solution)/shard_map/all_to_all | solution.py:97
  315.7 9.3 %copy-start.1 = (f32[4,128]{1,0:T(4,128)S(1)}, f32[4,128]{1,0:T(4,128)}, u32[]{:S(2)}) copy-start(f32[4,128]{1,0:T(4,128)} %param.12) | copy-start | bytes 6148
  316.2 25.4 %copy-start.5 = (bf16[2048,128]{1,0:T(8,128)(2,1)S(1)}, bf16[2048,128]{1,0:T(8,128)(2,1)}, u32[]{:S(2)}) copy-start(bf16[2048,128]{1,0:T(8,128)(2,1)} %param.14) | copy-start | bytes 1572868
  317.0 14.1 %all-to-all-start.2 = ((f32[8,4,2176]{2,1,0:T(4,128)}), f32[8,4,2176]{2,1,0:T(4,128)S(1)}, u32[]{:S(2)}, u32[]{:S(2)}) async-start(f32[8,4,2176]{2,1,0:T(4,128)} %copy.96), calls=%async_computation.2 | async-start | bytes 557056 | tf_op jit(solution)/shard_map/all_to_all | solution.py:125
  332.6 24.7 %all-to-all-start.3 = ((bf16[256,4,128]{2,1,0:T(4,128)(2,1)}), bf16[256,4,128]{2,1,0:T(4,128)(2,1)S(1)}, u32[]{:S(2)}, u32[]{:S(2)}) async-start(bf16[256,4,128]{2,1,0:T(4,128)(2,1)} %broadcast_in_dim.59), calls=%async_computation.3 | async-start | bytes 524288 | tf_op jit(solution)/shard_map/all_to_all | solution.py:135
